TPU v7x, 32 devices: a whole 2x2x4 slice. The times are simulated.
32 devices in a mesh: groups: 2 (over x), ctx: 16 (over z, y, core).
Axes of the slice: x: 2, y: 2, z: 4, core: 2. Of those that a mesh axis runs over, the one named last changes fastest.
Arguments:
- q_latent: bfloat16 [128, 1536], P(('groups', 'ctx')), parts along dimension 0, may hold values from -64 to 64
- q_gain: float32 [1536], replicated, may hold values from 0.1 to 1.9
- w_uq: bfloat16 [1536, 24576], P(None, 'ctx'), may hold values from -0.15625 to 0.15625
- w_uk: bfloat16 [128, 128, 512], P('ctx'), may hold values from -0.5 to 0.5
- w_uv: bfloat16 [128, 512, 128], P('ctx'), may hold values from -0.25 to 0.25
- w_o: bfloat16 [16384, 7168], P('ctx'), may hold values from -0.046875 to 0.046875
- latent_cache: bfloat16 [65536, 576], P(('groups', 'ctx')), parts along dimension 0, may hold values from -1024 to 1024
- kv_scales: float32 [65536, 4], P(('groups', 'ctx')), parts along dimension 0, may hold values from 0.5 to 2
- selected: int32 [128, 32], P(('groups', 'ctx')), parts along dimension 0, may hold values from 0 to 511, as said below
- counts: int32 [128], P(('groups', 'ctx')), parts along dimension 0, may hold values from 8 to 32
Outputs:
- attn_out: bfloat16 [128, 7168], P(('groups', 'ctx')), parts along dimension 0
There are 2 independent parts, one for each index of `groups`. A program takes and returns all parts, laid end to end along the dimension named above; an argument that names none is the same for every part. Nothing has to cross between parts.
Inputs may be any that keep to these rules, and one draw needn't show every extreme that they name: `selected`: each row lists 32 different block numbers. Over the rows 4 i to 4 i + 4 - 1 (the query tokens of one device) and their first counts entries, at most 8 different listed blocks lie in the range 32 j to 32 j + 31 for any j.
All inputs are finite; a program needn't handle non-finite values.
Results may differ from a plain program's by a relative error of at most 0.01.
The roundings to bfloat16 on the way count: a program that leaves them out, or rounds other values in their place, can miss the bound.
Values may be sent and summed in bfloat16 or wider, within the bound.
A program may use at most 128 MiB of HBM per device.

v0:
```python
import math
import jax
import jax.numpy as jnp
from jax import lax
from jax.sharding import PartitionSpec as P

BLK = 64
norm_eps = 1e-06
rope_base = 10000.0


def rotate_rotary(rotary, positions):
    half_width = rotary.shape[-1] // 2
    freq_index = jnp.arange(half_width, dtype=jnp.float32)
    inverse_freq = jnp.exp(freq_index * (-2.0 * math.log(rope_base) / rotary.shape[-1]))
    angles = positions[:, None] * inverse_freq[None, :]
    cosine = jnp.cos(angles)[:, None, :]
    sine = jnp.sin(angles)[:, None, :]
    first_half = rotary[:, :, :half_width]
    second_half = rotary[:, :, half_width:]
    return jnp.concatenate(
        [first_half * cosine - second_half * sine, first_half * sine + second_half * cosine], axis=2
    )


def local(q_latent, q_gain, w_uq, w_uk, w_uv, w_o, latent_cache, kv_scales, selected, counts):
    n_devices = lax.axis_size("ctx")
    heads_local = w_uk.shape[0]
    width_content = w_uk.shape[1]
    width_latent = w_uk.shape[2]
    width_rotary = latent_cache.shape[1] - width_latent
    width_row = width_latent + width_rotary
    q_local = q_latent.shape[0]
    top_blocks = selected.shape[1]
    block_len = BLK
    blocks_local = latent_cache.shape[0] // block_len
    blocks_total = blocks_local * n_devices
    capacity = max(2, 4 * top_blocks // n_devices)
    latent_f = q_latent.astype(jnp.float32)
    normed = (
        latent_f
        * lax.rsqrt(jnp.mean(latent_f * latent_f, axis=1, keepdims=True) + norm_eps)
        * q_gain
    ).astype(jnp.bfloat16)
    scaled = (
        latent_cache[:, :width_latent].astype(jnp.float32)
        * jnp.repeat(kv_scales, width_latent // kv_scales.shape[1], axis=1)
    ).astype(jnp.bfloat16)
    cache_blocks = jnp.concatenate([scaled, latent_cache[:, width_latent:]], axis=1).reshape(
        blocks_local, block_len, width_row
    )
    live_sel = jnp.arange(top_blocks, dtype=jnp.int32)[None, :] < counts[:, None]
    block_match = selected[:, :, None] == jnp.arange(blocks_total, dtype=jnp.int32)[None, None, :]
    needed = (
        jnp.any(block_match & live_sel[:, :, None], axis=(0, 1))
        .reshape(n_devices, blocks_local)
        .astype(jnp.int32)
    )
    order_rank = jnp.cumsum(needed, axis=1) - 1
    slot_match = (needed[:, :, None] == 1) & (
        order_rank[:, :, None] == jnp.arange(capacity, dtype=jnp.int32)[None, None, :]
    )
    requests = jnp.sum(
        jnp.where(slot_match, jnp.arange(blocks_local, dtype=jnp.int32)[None, :, None], 0), axis=1
    )
    rank_flat = order_rank.reshape(blocks_total)
    sel_rank = jnp.sum(jnp.where(block_match, rank_flat[None, None, :], 0), axis=2)
    slot_index = jnp.where(live_sel, selected // blocks_local * capacity + sel_rank, 0)
    shard_piece = lax.all_gather(normed, "ctx", axis=0, tiled=True)
    row_count = shard_piece.shape[0]
    projected = jnp.dot(shard_piece, w_uq, preferred_element_type=jnp.float32).reshape(
        row_count, heads_local, width_content + width_rotary
    )
    content = projected[:, :, :width_content].astype(jnp.bfloat16)
    positions = jnp.arange(row_count, dtype=jnp.int32).astype(jnp.float32)
    rotated = rotate_rotary(projected[:, :, width_content:], positions).astype(jnp.bfloat16)
    absorbed = jnp.einsum("khn,hnc->khc", content, w_uk, preferred_element_type=jnp.float32).astype(
        jnp.bfloat16
    )
    head_queries = jnp.concatenate([absorbed, rotated], axis=2)
    queries = lax.all_to_all(head_queries, "ctx", split_axis=0, concat_axis=1, tiled=True)
    served = cache_blocks[lax.all_to_all(requests, "ctx", split_axis=0, concat_axis=0, tiled=True)]
    fetched = lax.all_to_all(served, "ctx", split_axis=0, concat_axis=0, tiled=True)
    fetched_rows = fetched.reshape(n_devices * capacity * block_len, width_row)
    token_index = (
        slot_index[:, :, None] * block_len + jnp.arange(block_len, dtype=jnp.int32)[None, None, :]
    ).reshape(q_local, top_blocks * block_len)
    live_tokens = jnp.repeat(live_sel, block_len, axis=1)
    softmax_scale = 1.0 / math.sqrt(width_content + width_rotary)

    def attend(inputs):
        query_row, token_rows, live_row = inputs
        key_rows = fetched_rows[token_rows]
        scores = jnp.dot(query_row, key_rows.T, preferred_element_type=jnp.float32) * softmax_scale
        scores = jnp.where(live_row[None, :], scores, -jnp.inf)
        row_peak = jnp.max(scores, axis=1, keepdims=True)
        exponent = jnp.exp(scores - row_peak)
        weights = (exponent / jnp.sum(exponent, axis=1, keepdims=True)).astype(jnp.bfloat16)
        return jnp.dot(
            weights, key_rows[:, :width_latent], preferred_element_type=jnp.float32
        ).astype(jnp.bfloat16)

    latent_out = lax.map(attend, (queries, token_index, live_tokens))
    head_out = lax.all_to_all(latent_out, "ctx", split_axis=1, concat_axis=0, tiled=True)
    head_values = jnp.einsum(
        "qhc,hcv->qhv", head_out, w_uv, preferred_element_type=jnp.float32
    ).astype(jnp.bfloat16)
    head_values = head_values.reshape(head_values.shape[0], heads_local * w_uv.shape[2])
    return lax.psum_scatter(
        jnp.dot(head_values, w_o, preferred_element_type=jnp.float32),
        "ctx",
        scatter_dimension=0,
        tiled=True,
    ).astype(jnp.bfloat16)


def solution(mesh):
    in_specs = (
        P(("groups", "ctx"), None),
        P(),
        P(None, "ctx"),
        P("ctx", None, None),
        P("ctx", None, None),
        P("ctx", None),
        P(("groups", "ctx"), None),
        P(("groups", "ctx"), None),
        P(("groups", "ctx"), None),
        P(("groups", "ctx")),
    )
    out_specs = P(("groups", "ctx"), None)
    return jax.shard_map(local, mesh=mesh, in_specs=in_specs, out_specs=out_specs, check_vma=False)
```

profile of v0, /device:TPU:0, one launch (start us, length us, event | category | flops | bytes accessed | tf_op | source)
XLA Modules:
  0.0 466.6 jit_solution(13454047989507777395)
XLA Ops:
  2.9 7.4 %all-to-all-start.1 = ((s32[16,1,8]{2,1,0:T(1,128)}), s32[16,1,8]{2,1,0:T(1,128)S(1)}, u32[]{:S(2)}, u32[]{:S(2)}) async-start(s32[16,1,8]{2,1,0:T(1,128)} %bitcast.18), calls=%async_computation.1 | async-start | bytes 16384 | tf_op jit(solution)/shard_map/all_to_all | solution.py:82
  12.0 22.2 %all-gather = bf16[16,4,1536]{2,1,0:T(4,128)(2,1)S(1)} all-gather(bf16[1,4,1536]{2,1,0:T(4,128)(2,1)S(1)} %fusion.30), channel_id=1, replica_groups=mesh['groups'=2,'ctx'=16] {'ctx'}, dimensions={0}, use_global_device_ids=true | all-gather | bytes 208896 | tf_op jit(solution)/shard_map/all_gather | solution.py:69
  34.2 3.3 fusion.39
  38.6 1.2 copy.45
  40.4 2.5 copy.59
  42.9 1.0 copy.60
  44.0 4.3 all-to-all-start
  48.2 4.7 %broadcast_in_dim.79 = f32[2048,4,128]{2,1,0:T(4,128)S(1)} broadcast(f32[2048,4]{1,0:T(8,128)S(1)} %copy.48), dimensions={0,1} | broadcast | bytes 4227072 | tf_op jit(solution)/shard_map/broadcast_in_dim | solution.py:47
  54.5 7.6 %gather_fusion.1 = bf16[128,64,576]{2,1,0:T(8,128)(2,1)} fusion(bf16[32,64,576]{2,1,0:T(8,128)(2,1)S(1)} %bitcast.67, s32[1024]{0:T(1024)S(1)} %pad_clamp_fusion), kind=kCustom, calls=%fused_computation.1 | custom fusion | bytes 18874880 | tf_op jit(solution)/shard_map/gather | solution.py:82
  62.1 2.7 all-to-all-done
  64.8 5.1 %all-to-all-start.2 = ((bf16[16,8,64,576]{3,2,1,0:T(8,128)(2,1)}), bf16[16,8,64,576]{3,2,1,0:T(8,128)(2,1)}, u32[]{:S(2)}, u32[]{:S(2)}) async-start(bf16[16,8,64,576]{3,2,1,0:T(8,128)(2,1)} %bitcast.68), calls=%async_computation.2 | async-start | bytes 20971520 | tf_op jit(solution)/shard_map/all_to_all | solution.py:83
  70.8 1.1 copy.79
  72.0 184.8 %all-to-all-done.2 = bf16[16,8,64,576]{3,2,1,0:T(8,128)(2,1)} async-done(((bf16[16,8,64,576]{3,2,1,0:T(8,128)(2,1)}), bf16[16,8,64,576]{3,2,1,0:T(8,128)(2,1)}, u32[]{:S(2)}, u32[]{:S(2)}) %all-to-all-start.2) | async-done | bytes 9437216 | tf_op jit(solution)/shard_map/all_to_all | solution.py:83
  256.8 63.6 %while.10 = (s32[]{:T(128)}, bf16[4,128,512]{2,1,0:T(8,128)(2,1)}, pred[4,2048]{1,0:T(4,128)(4,1)S(1)}, bf16[4,128,576]{2,1,0:T(8,128)(2,1)S(1)}, s32[4,2048]{1,...) while((s32[]{:T(128)}, bf16[4,128,512]{2,1,0:T(8,128)(2,1)}, pred[4,2048]{1,0:T(4,128)(4,1)S(1)}, ...), condition=%wide.region_8.9_spmd, body=%wide.region_5.8_spmd.sunk | while | flops 572595968 | bytes 12928089 | solution.py:103
  256.8 13.3 %gather_fusion = bf16[2048,576]{1,0:T(8,128)(2,1)S(1)} fusion(bf16[8192,576]{1,0:T(8,128)(2,1)} %get-tuple-element.118, s32[2048]{0:T(1024)S(1)} %broadcast_clamp_fusion.2), kind=kCustom, calls=%fused_computation.clone.1 | custom fusion | bytes 4726784 | tf_op jit(solution)/shard_map/while/body/eval_jaxpr/gather | solution.py:93
  270.2 1.1 fusion.54
  271.5 1.2 fusion.56
  272.8 13.3 %gather_fusion = bf16[2048,576]{1,0:T(8,128)(2,1)S(1)} fusion(bf16[8192,576]{1,0:T(8,128)(2,1)} %get-tuple-element.118, s32[2048]{0:T(1024)S(1)} %broadcast_clamp_fusion.2), kind=kCustom, calls=%fused_computation.clone.1 | custom fusion | bytes 4726784 | tf_op jit(solution)/shard_map/while/body/eval_jaxpr/gather | solution.py:93
  286.1 1.1 fusion.54
  287.5 1.2 fusion.56
  288.7 13.3 %gather_fusion = bf16[2048,576]{1,0:T(8,128)(2,1)S(1)} fusion(bf16[8192,576]{1,0:T(8,128)(2,1)} %get-tuple-element.118, s32[2048]{0:T(1024)S(1)} %broadcast_clamp_fusion.2), kind=kCustom, calls=%fused_computation.clone.1 | custom fusion | bytes 4726784 | tf_op jit(solution)/shard_map/while/body/eval_jaxpr/gather | solution.py:93
  302.0 1.1 fusion.54
  303.4 1.2 fusion.56
  304.6 13.3 %gather_fusion = bf16[2048,576]{1,0:T(8,128)(2,1)S(1)} fusion(bf16[8192,576]{1,0:T(8,128)(2,1)} %get-tuple-element.118, s32[2048]{0:T(1024)S(1)} %broadcast_clamp_fusion.2), kind=kCustom, calls=%fused_computation.clone.1 | custom fusion | bytes 4726784 | tf_op jit(solution)/shard_map/while/body/eval_jaxpr/gather | solution.py:93
  317.9 1.1 fusion.54
  319.3 1.2 fusion.56
  320.4 2.3 copy.54
  322.8 45.6 %all-to-all-start.3 = ((bf16[4,128,512]{2,0,1:T(4,128)(2,1)}), bf16[4,128,512]{2,0,1:T(4,128)(2,1)S(1)}, u32[]{:S(2)}, u32[]{:S(2)}) async-start(bf16[4,128,512]{2,0,1:T(4,128)(2,1)} %copy.54), calls=%async_computation.3 | async-start | bytes 1048576 | tf_op jit(solution)/shard_map/all_to_all | solution.py:104
  369.7 13.0 %all-to-all-done.3 = bf16[4,128,512]{2,0,1:T(4,128)(2,1)S(1)} async-done(((bf16[4,128,512]{2,0,1:T(4,128)(2,1)}), bf16[4,128,512]{2,0,1:T(4,128)(2,1)S(1)}, u32[]{:S(2)}, u32[]{:S(2)}) %all-to-all-start.3) | async-done | bytes 524320 | tf_op jit(solution)/shard_map/all_to_all | solution.py:104
  383.3 8.0 %fusion.23 = f32[64,7168]{1,0:T(8,128)S(1)} fusion(bf16[1024,7168]{1,0:T(8,128)(2,1)} %param.17, bf16[8,8,8,128]{3,2,1,0:T(8,128)(2,1)S(1)} %fusion.20), kind=kOutput, calls=%fused_computation.37 | convolution fusion | flops 939524096 | bytes 16646144 | tf_op jit(solution)/shard_map/dot_general | solution.py:110
  391.3 73.7 %all-reduce.2 = bf16[64,7168]{1,0:T(8,128)(2,1)} all-reduce(f32[64,7168]{1,0:T(8,128)S(1)} %fusion.23), channel_id=2, replica_groups=mesh['groups'=2,'ctx'=16] {'ctx'}, use_global_device_ids=true, to_apply=%region_9.10.clone | all-reduce | flops 458752 | bytes 2752512
  465.1 1.6 dynamic-slice_convert_fusion
  (83 shorter events, 11.2 us)
Async XLA Ops:
  0.0 38.0 %copy-start = (bf16[8,128,512]{2,1,0:T(8,128)(2,1)S(1)}, bf16[8,128,512]{2,1,0:T(8,128)(2,1)}, u32[]{:S(2)}) copy-start(bf16[8,128,512]{2,1,0:T(8,128)(2,1)} %param.15) | copy-start | bytes 3145732
  2.9 41.1 %all-to-all-start.1 = ((s32[16,1,8]{2,1,0:T(1,128)}), s32[16,1,8]{2,1,0:T(1,128)S(1)}, u32[]{:S(2)}, u32[]{:S(2)}) async-start(s32[16,1,8]{2,1,0:T(1,128)} %bitcast.18), calls=%async_computation.1 | async-start | bytes 16384 | tf_op jit(solution)/shard_map/all_to_all | solution.py:82
  38.6 1.2 copy-start.5
  38.6 1.8 slice-start
  39.8 3.1 slice-start.1
  44.0 20.9 %all-to-all-start = ((bf16[64,8,576]{2,1,0:T(8,128)(2,1)}), bf16[64,8,576]{2,1,0:T(8,128)(2,1)}, u32[]{:S(2)}, u32[]{:S(2)}) async-start(bf16[64,8,576]{2,1,0:T(8,128)(2,1)} %copy.45), calls=%async_computation | async-start | bytes 1310720 | tf_op jit(solution)/shard_map/all_to_all | solution.py:81
  48.2 4.7 %copy-start.2 = (bf16[2048,512]{1,0:T(8,128)(2,1)S(1)}, bf16[2048,512]{1,0:T(8,128)(2,1)}, u32[]{:S(2)}) copy-start(bf16[2048,512]{1,0:T(8,128)(2,1)} %copy.59) | copy-start | bytes 6291460
  52.9 1.0 copy-start.3
  64.8 5.2 %copy-start.6 = (s32[4,32]{1,0:T(4,128)S(1)}, s32[4,32]{1,0:T(4,128)}, u32[]{:S(2)}) copy-start(s32[4,32]{1,0:T(4,128)} %param.20) | copy-start | bytes 1540
  64.8 5.5 %copy-start.7 = (s32[4]{0:T(128)S(1)}, s32[4]{0:T(128)}, u32[]{:S(2)}) copy-start(s32[4]{0:T(128)} %param.21) | copy-start | bytes 52
  64.8 192.0 %all-to-all-start.2 = ((bf16[16,8,64,576]{3,2,1,0:T(8,128)(2,1)}), bf16[16,8,64,576]{3,2,1,0:T(8,128)(2,1)}, u32[]{:S(2)}, u32[]{:S(2)}) async-start(bf16[16,8,64,576]{3,2,1,0:T(8,128)(2,1)} %bitcast.68), calls=%async_computation.2 | async-start | bytes 20971520 | tf_op jit(solution)/shard_map/all_to_all | solution.py:83
  256.8 111.6 %copy-start.8 = (u32[32]{0:T(128)S(1)}, u32[32]{0:T(128)}, u32[]{:S(2)}) copy-start(u32[32]{0:T(128)} %constant.72) | copy-start | bytes 388
  320.4 62.6 %copy-start.4 = (bf16[8,512,128]{2,1,0:T(8,128)(2,1)S(1)}, bf16[8,512,128]{2,1,0:T(8,128)(2,1)}, u32[]{:S(2)}) copy-start(bf16[8,512,128]{2,1,0:T(8,128)(2,1)} %param.16) | copy-start | bytes 3145732
  322.8 59.9 %all-to-all-start.3 = ((bf16[4,128,512]{2,0,1:T(4,128)(2,1)}), bf16[4,128,512]{2,0,1:T(4,128)(2,1)S(1)}, u32[]{:S(2)}, u32[]{:S(2)}) async-start(bf16[4,128,512]{2,0,1:T(4,128)(2,1)} %copy.54), calls=%async_computation.3 | async-start | bytes 1048576 | tf_op jit(solution)/shard_map/all_to_all | solution.py:104
  383.3 83.3 %copy-start.1 = (bf16[8,128,512]{2,1,0:T(8,128)(2,1)S(1)}, bf16[8,128,512]{2,1,0:T(8,128)(2,1)}, u32[]{:S(2)}) copy-start(bf16[8,128,512]{2,1,0:T(8,128)(2,1)} %param.15) | copy-start | bytes 3145732
where the time goes:
time: 468 us; the launch traced here: 467 us
  waiting for transfers between devices  201 us (43%)
  blocking collectives  95.9 us (20%)
  local copies, waits for them, and re-layouts  78.1 us (17%)
  starting transfers between devices  62.5 us (13%)
  matrix products  20.8 us (4%)
  other arithmetic  7.66 us (2%)
    all_to_all x1, waiting for transfers between devices, local(): lax.all_to_all(served, 'ctx', split_axis=0, concat_axis=0, tiled=True)  185 us
    unnamed x1, blocking collectives  73.7 us
    gather x4, local copies, waits for them, and re-layouts, attend(): key_rows = fetched_rows[token_rows]  53.1 us
    all_to_all x1, starting transfers between devices, local(): lax.all_to_all(latent_out, 'ctx', split_axis=1, concat_axis=0, tiled=True)  45.6 us
    all_gather x1, blocking collectives, local(): shard_piece = lax.all_gather(normed, 'ctx', axis=0, tiled=True)  22.2 us
    all_to_all x1, waiting for transfers between devices, local(): lax.all_to_all(latent_out, 'ctx', split_axis=1, concat_axis=0, tiled=True)  13 us
  transfers between devices with their start and end apart: 4, of which 3 were waited for; matrix products, arithmetic and copies ran while one was open for 6% of the time, Pallas kernels for 0%

commit v1 on v0

--- a/solution.py
+++ b/solution.py
@@ -7,6 +7,20 @@
 BLK = 64
 norm_eps = 1e-06
 rope_base = 10000.0
+
+
+def outputs_pair(field_in, at_axis, piece_in):
+    value_now = field_in.shape
+    built = field_in.reshape(
+        *value_now[:at_axis], piece_in, value_now[at_axis] // piece_in, *value_now[at_axis + 1 :]
+    )
+    return jnp.moveaxis(built, at_axis, 0)
+
+
+def shape_counts(body, on_dim):
+    body = jnp.moveaxis(body, 0, on_dim)
+    carry = body.shape
+    return body.reshape(*carry[:on_dim], carry[on_dim] * carry[on_dim + 1], *carry[on_dim + 2 :])
 
 
 def rotate_rotary(rotary, positions):
@@ -80,7 +94,19 @@
     head_queries = jnp.concatenate([absorbed, rotated], axis=2)
     queries = lax.all_to_all(head_queries, "ctx", split_axis=0, concat_axis=1, tiled=True)
     served = cache_blocks[lax.all_to_all(requests, "ctx", split_axis=0, concat_axis=0, tiled=True)]
-    fetched = lax.all_to_all(served, "ctx", split_axis=0, concat_axis=0, tiled=True)
+    shaped = lax.axis_size("ctx")
+    t_next = lax.axis_index("ctx")
+    frame_out, oldest = (shaped, t_next)
+    step_out = outputs_pair(served, 0, frame_out)
+    lower = step_out
+    for no in range(1, frame_out):
+        v1, last = ((oldest + no) % frame_out, (oldest - no) % frame_out)
+        all_values = lax.dynamic_index_in_dim(step_out, v1, 0)
+        wide_out = lax.ppermute(
+            all_values, "ctx", [(b, (b + no) % frame_out) for b in range(frame_out)]
+        )
+        lower = lax.dynamic_update_slice_in_dim(lower, wide_out, last, axis=0)
+    fetched = shape_counts(lower, 0)
     fetched_rows = fetched.reshape(n_devices * capacity * block_len, width_row)
     token_index = (
         slot_index[:, :, None] * block_len + jnp.arange(block_len, dtype=jnp.int32)[None, None, :]

time: 468 us -> 523 us (1.12)
  waiting for transfers between devices: 201 us -> 125 us
  starting transfers between devices: 62.5 us -> 131 us
  local copies, waits for them, and re-layouts: 78.1 us -> 118 us
  matrix products: 20.8 us -> 32.3 us
  other arithmetic: 7.66 us -> 15.8 us
    all_to_all x1 -> x0, waiting for transfers between devices: 185 us -> none  [local(): lax.all_to_all(served, 'ctx', split_axis=0, concat_axis=0, tiled=True)]
    ppermute x0 -> x15, waiting for transfers between devices: none -> 112 us  [local(): lax.ppermute(all_values, 'ctx', [(b, (b + no) % frame_out) for b in range...]
    ppermute x0 -> x15, starting transfers between devices: none -> 107 us  [local(): lax.ppermute(all_values, 'ctx', [(b, (b + no) % frame_out) for b in range...]
    all_to_all x1, starting transfers between devices: 45.6 us -> 12.5 us  [local(): lax.all_to_all(latent_out, 'ctx', split_axis=1, concat_axis=0, tiled=True)]
    dynamic_update_slice x0 -> x15, local copies, waits for them, and re-layouts: none -> 19.2 us  [local(): lower = lax.dynamic_update_slice_in_dim(lower, wide_out, last, axis=0)]
    dot_general x4, matrix products: 4.26 us -> 11.3 us  [attend(): jnp.dot(query_row, key_rows.T, preferred_element_type=jnp.float32)]
    dynamic_slice x0 -> x1, local copies, waits for them, and re-layouts: none -> 6.91 us  [local(): all_values = lax.dynamic_index_in_dim(step_out, v1, 0)]
    gather x4, local copies, waits for them, and re-layouts: 53.1 us -> 59.6 us  [attend(): key_rows = fetched_rows[token_rows]]
  transfers between devices with their start and end apart: 4 -> 18, of which waited for: 3 -> 5; matrix products, arithmetic and copies ran while one was open for 6% -> 13% of each run, Pallas kernels for 0% -> 0%
where the time goes in v1:
time: 523 us; the launch traced here: 521 us
  starting transfers between devices  131 us (25%)
  waiting for transfers between devices  125 us (24%)
  local copies, waits for them, and re-layouts  118 us (23%)
  blocking collectives  97.5 us (19%)
  matrix products  32.3 us (6%)
  other arithmetic  15.8 us (3%)
    ppermute x15, waiting for transfers between devices, local(): lax.ppermute(all_values, 'ctx', [(b, (b + no) % frame_out) for b in range...  112 us
    ppermute x15, starting transfers between devices, local(): lax.ppermute(all_values, 'ctx', [(b, (b + no) % frame_out) for b in range...  107 us
    unnamed x1, blocking collectives  74 us
    gather x4, local copies, waits for them, and re-layouts, attend(): key_rows = fetched_rows[token_rows]  59.6 us
    all_gather x1, blocking collectives, local(): shard_piece = lax.all_gather(normed, 'ctx', axis=0, tiled=True)  23.4 us
    dynamic_update_slice x15, local copies, waits for them, and re-layouts, local(): lower = lax.dynamic_update_slice_in_dim(lower, wide_out, last, axis=0)  19.2 us
    all_to_all x1, waiting for transfers between devices, local(): lax.all_to_all(latent_out, 'ctx', split_axis=1, concat_axis=0, tiled=True)  13 us
    all_to_all x1, starting transfers between devices, local(): lax.all_to_all(latent_out, 'ctx', split_axis=1, concat_axis=0, tiled=True)  12.5 us
  transfers between devices with their start and end apart: 18, of which 5 were waited for; matrix products, arithmetic and copies ran while one was open for 13% of the time, Pallas kernels for 0%

profile of v1, /device:TPU:0, one launch (start us, length us, event | category | flops | bytes accessed | tf_op | source)
XLA Modules:
  0.0 520.9 jit_solution(3416876795139151567)
XLA Ops:
  3.1 7.4 %all-to-all-start.1 = ((s32[16,1,8]{2,1,0:T(1,128)}), s32[16,1,8]{2,1,0:T(1,128)S(1)}, u32[]{:S(2)}, u32[]{:S(2)}) async-start(s32[16,1,8]{2,1,0:T(1,128)} %bitcast.34), calls=%async_computation.1 | async-start | bytes 16384 | tf_op jit(solution)/shard_map/all_to_all | solution.py:96
  13.5 23.4 %all-gather = bf16[16,4,1536]{2,1,0:T(4,128)(2,1)} all-gather(bf16[1,4,1536]{2,1,0:T(4,128)(2,1)S(1)} %fusion.30), channel_id=1, replica_groups=mesh['groups'=2,'ctx'=16] {'ctx'}, dimensions={0}, use_global_device_ids=true | all-gather | bytes 208896 | tf_op jit(solution)/shard_map/all_gather | solution.py:83
  38.6 4.1 fusion.39
  49.7 2.5 copy.74
  52.7 5.0 broadcast_in_dim.79
  57.8 2.4 fusion.18
  64.0 3.6 all-to-all-start
  67.9 9.5 %gather_fusion.1 = bf16[128,64,576]{2,1,0:T(8,128)(2,1)} fusion(bf16[32,64,576]{2,1,0:T(8,128)(2,1)} %bitcast.101, s32[1024]{0:T(1024)S(1)} %pad_clamp_fusion), kind=kCustom, calls=%fused_computation.1 | custom fusion | bytes 18874880 | tf_op jit(solution)/shard_map/gather | solution.py:96
  77.4 6.9 %dynamic-slice_bitcast_fusion = (bf16[1,1,8,64,576]{4,3,2,0,1:T(8,128)(2,1)S(1)}, bf16[1,1,8,64,576]{4,3,2,0,1:T(8,128)(2,1)S(1)}, bf16[1,1,8,64,576]{4,3,2,0,1:...) fusion(bf16[16,8,64,576]{3,2,1,0:T(8,128)(2,1)} %bitcast.98, ...), kind=kLoop, calls=%fused_computation.29 | loop fusion | bytes 17694780 | tf_op jit(solution)/shard_map/jit(dynamic_index_in_dim)/dynamic_slice | solution.py:104
  91.2 12.4 %collective-permute-done = bf16[1,1,8,64,576]{4,3,2,0,1:T(8,128)(2,1)} collective-permute-done((bf16[1,1,8,64,576]{4,3,2,0,1:T(8,128)(2,1)}, bf16[1,1,8,64,576]{4,3,2,0,1:T(8,128)(2,1)}, u32[]{:S(2)}, u32[]{:S(2)}) %collective-permute-start) | collective-permute-done | bytes 589856 | tf_op jit(solution)/shard_map/ppermute | solution.py:105
  105.6 11.4 %collective-permute-start.6 = (bf16[1,1,8,64,576]{4,3,2,0,1:T(8,128)(2,1)}, bf16[1,1,8,64,576]{4,3,2,0,1:T(8,128)(2,1)S(1)}, u32[]{:S(2)}, u32[]{:S(2)}) collective-permute-start(bf16[1,1,8,64,576]{4,3,2,0,1:T(8,128)(2,1)} %get-tuple-element.59), channel_id=1, source_target_pairs={{0,7},{1,8},{2,9},{3,10},{4,11},{5,12},{6,13},{7,14},{8,15},{9,0},... | collective-permute-start | bytes 1769480 | tf_op jit(solution)/shard_map/ppermute | solution.py:105
  119.0 2.4 collective-permute-start.7
  125.7 90.9 %collective-permute-done.4 = bf16[1,1,8,64,576]{4,3,2,0,1:T(8,128)(2,1)} collective-permute-done((bf16[1,1,8,64,576]{4,3,2,0,1:T(8,128)(2,1)}, bf16[1,1,8,64,576]{4,3,2,0,1:T(8,128)(2,1)}, u32[]{:S(2)}, u32[]{:S(2)}) %collective-permute-start.4) | collective-permute-done | bytes 589856 | tf_op jit(solution)/shard_map/ppermute | solution.py:105
  218.7 15.5 %collective-permute-start.10 = (bf16[1,1,8,64,576]{4,3,2,0,1:T(8,128)(2,1)}, bf16[1,1,8,64,576]{4,3,2,0,1:T(8,128)(2,1)S(1)}, u32[]{:S(2)}, u32[]{:S(2)}) collective-permute-start(bf16[1,1,8,64,576]{4,3,2,0,1:T(8,128)(2,1)} %get-tuple-element.55), channel_id=1, source_target_pairs={{0,11},{1,12},{2,13},{3,14},{4,15},{5,0},{6,1},{7,2},{8,3},{9,4},{... | collective-permute-start | bytes 1769480 | tf_op jit(solution)/shard_map/ppermute | solution.py:105
  235.1 31.6 %collective-permute-start.11 = (bf16[1,1,8,64,576]{4,3,2,0,1:T(8,128)(2,1)}, bf16[1,1,8,64,576]{4,3,2,0,1:T(8,128)(2,1)S(1)}, u32[]{:S(2)}, u32[]{:S(2)}) collective-permute-start(bf16[1,1,8,64,576]{4,3,2,0,1:T(8,128)(2,1)} %get-tuple-element.54), channel_id=1, source_target_pairs={{0,12},{1,13},{2,14},{3,15},{4,0},{5,1},{6,2},{7,3},{8,4},{9,5},{1... | collective-permute-start | bytes 1769480 | tf_op jit(solution)/shard_map/ppermute | solution.py:105
  269.7 20.7 %collective-permute-start.13 = (bf16[1,1,8,64,576]{4,3,2,0,1:T(8,128)(2,1)S(1)}, bf16[1,1,8,64,576]{4,3,2,0,1:T(8,128)(2,1)S(1)}, u32[]{:S(2)}, u32[]{:S(2)}) collective-permute-start(bf16[1,1,8,64,576]{4,3,2,0,1:T(8,128)(2,1)S(1)} %get-tuple-element.66), channel_id=1, source_target_pairs={{0,14},{1,15},{2,0},{3,1},{4,2},{5,3},{6,4},{7,5},{8,6},{9,7},{10,... | collective-permute-start | bytes 1769480 | tf_op jit(solution)/shard_map/ppermute | solution.py:105
  291.3 18.8 %collective-permute-start.14 = (bf16[1,1,8,64,576]{4,3,2,0,1:T(8,128)(2,1)S(1)}, bf16[1,1,8,64,576]{4,3,2,0,1:T(8,128)(2,1)S(1)}, u32[]{:S(2)}, u32[]{:S(2)}) collective-permute-start(bf16[1,1,8,64,576]{4,3,2,0,1:T(8,128)(2,1)S(1)} %get-tuple-element.52), channel_id=1, source_target_pairs={{0,15},{1,0},{2,1},{3,2},{4,3},{5,4},{6,5},{7,6},{8,7},{9,8},{10,9... | collective-permute-start | bytes 1769480 | tf_op jit(solution)/shard_map/ppermute | solution.py:105
  313.7 4.6 collective-permute-done.13
  319.2 4.5 collective-permute-done.14
  324.7 84.0 %while.10 = (s32[]{:T(128)}, bf16[4,128,512]{2,1,0:T(8,128)(2,1)S(1)}, pred[4,2048]{1,0:T(4,128)(4,1)S(1)}, bf16[4,128,576]{2,1,0:T(8,128)(2,1)S(1)}, s32[4,2048...) while((s32[]{:T(128)}, bf16[4,128,512]{2,1,0:T(8,128)(2,1)S(1)}, pred[4,2048]{1,0:T(4,128)(4,1)S(1)}, ...), condition=%wide.region_8.9_spmd, body=%wide.region_5.8_spmd.sunk | while | flops 572595968 | bytes 12665945 | solution.py:129
  325.6 14.9 %gather_fusion = bf16[2048,576]{1,0:T(8,128)(2,1)} fusion(bf16[8192,576]{1,0:T(8,128)(2,1)} %get-tuple-element.133, s32[2048]{0:T(1024)S(1)} %broadcast_clamp_fusion.2), kind=kCustom, calls=%fused_computation.clone.1 | custom fusion | bytes 4726784 | tf_op jit(solution)/shard_map/while/body/eval_jaxpr/gather | solution.py:119
  340.6 2.8 fusion.54
  346.6 14.9 %gather_fusion = bf16[2048,576]{1,0:T(8,128)(2,1)} fusion(bf16[8192,576]{1,0:T(8,128)(2,1)} %get-tuple-element.133, s32[2048]{0:T(1024)S(1)} %broadcast_clamp_fusion.2), kind=kCustom, calls=%fused_computation.clone.1 | custom fusion | bytes 4726784 | tf_op jit(solution)/shard_map/while/body/eval_jaxpr/gather | solution.py:119
  361.5 2.8 fusion.54
  367.6 14.9 %gather_fusion = bf16[2048,576]{1,0:T(8,128)(2,1)} fusion(bf16[8192,576]{1,0:T(8,128)(2,1)} %get-tuple-element.133, s32[2048]{0:T(1024)S(1)} %broadcast_clamp_fusion.2), kind=kCustom, calls=%fused_computation.clone.1 | custom fusion | bytes 4726784 | tf_op jit(solution)/shard_map/while/body/eval_jaxpr/gather | solution.py:119
  382.5 2.8 fusion.54
  388.6 14.9 %gather_fusion = bf16[2048,576]{1,0:T(8,128)(2,1)} fusion(bf16[8192,576]{1,0:T(8,128)(2,1)} %get-tuple-element.133, s32[2048]{0:T(1024)S(1)} %broadcast_clamp_fusion.2), kind=kCustom, calls=%fused_computation.clone.1 | custom fusion | bytes 4726784 | tf_op jit(solution)/shard_map/while/body/eval_jaxpr/gather | solution.py:119
  403.5 2.8 fusion.54
  409.9 12.5 %all-to-all-start.2 = ((bf16[4,128,512]{2,0,1:T(4,128)(2,1)}), bf16[4,128,512]{2,0,1:T(4,128)(2,1)S(1)}, u32[]{:S(2)}, u32[]{:S(2)}) async-start(bf16[4,128,512]{2,0,1:T(4,128)(2,1)} %copy.69), calls=%async_computation.2 | async-start | bytes 1048576 | tf_op jit(solution)/shard_map/all_to_all | solution.py:130
  423.7 13.0 %all-to-all-done.2 = bf16[4,128,512]{2,0,1:T(4,128)(2,1)S(1)} async-done(((bf16[4,128,512]{2,0,1:T(4,128)(2,1)}), bf16[4,128,512]{2,0,1:T(4,128)(2,1)S(1)}, u32[]{:S(2)}, u32[]{:S(2)}) %all-to-all-start.2) | async-done | bytes 524320 | tf_op jit(solution)/shard_map/all_to_all | solution.py:130
  437.4 7.9 %fusion.23 = f32[64,7168]{1,0:T(8,128)S(1)} fusion(bf16[1024,7168]{1,0:T(8,128)(2,1)} %param.17, bf16[8,8,8,128]{3,2,1,0:T(8,128)(2,1)S(1)} %fusion.20), kind=kOutput, calls=%fused_computation.52 | convolution fusion | flops 939524096 | bytes 16646144 | tf_op jit(solution)/shard_map/dot_general | solution.py:136
  445.3 74.0 %all-reduce.2 = bf16[64,7168]{1,0:T(8,128)(2,1)} all-reduce(f32[64,7168]{1,0:T(8,128)S(1)} %fusion.23), channel_id=2, replica_groups=mesh['groups'=2,'ctx'=16] {'ctx'}, use_global_device_ids=true, to_apply=%region_9.10.clone | all-reduce | flops 458752 | bytes 2752512
  (133 shorter events, 63.4 us)
Async XLA Ops:
  0.0 62.2 %copy-start = (bf16[8,128,512]{2,1,0:T(8,128)(2,1)S(1)}, bf16[8,128,512]{2,1,0:T(8,128)(2,1)}, u32[]{:S(2)}) copy-start(bf16[8,128,512]{2,1,0:T(8,128)(2,1)} %param.15) | copy-start | bytes 3145732
  0.0 52.5 %copy-start.5 = (s32[4,32]{1,0:T(4,128)S(1)}, s32[4,32]{1,0:T(4,128)}, u32[]{:S(2)}) copy-start(s32[4,32]{1,0:T(4,128)} %param.20) | copy-start | bytes 1540
  0.0 49.7 %slice-start = ((bf16[2048,576]{0,1:T(8,128)(2,1)}), bf16[2048,512]{0,1:T(8,128)(2,1)S(1)}, s32[]{:S(2)}) async-start(bf16[2048,576]{0,1:T(8,128)(2,1)} %param.18), calls=%async_computation.3 | async-start | bytes 4194304 | tf_op jit(solution)/shard_map/slice | solution.py:60
  0.0 52.2 %slice-start.1 = ((bf16[2048,576]{0,1:T(8,128)(2,1)}), bf16[2048,64]{0,1:T(8,128)(2,1)S(1)}, s32[]{:S(2)}) async-start(bf16[2048,576]{0,1:T(8,128)(2,1)} %param.18), calls=%async_computation.4 | async-start | bytes 524288 | tf_op jit(solution)/shard_map/slice | solution.py:63
  0.9 1.0 copy-start.6
  3.1 60.9 %all-to-all-start.1 = ((s32[16,1,8]{2,1,0:T(1,128)}), s32[16,1,8]{2,1,0:T(1,128)S(1)}, u32[]{:S(2)}, u32[]{:S(2)}) async-start(s32[16,1,8]{2,1,0:T(1,128)} %bitcast.34), calls=%async_computation.1 | async-start | bytes 16384 | tf_op jit(solution)/shard_map/all_to_all | solution.py:96
  52.2 9.8 %copy-start.8 = (f32[64]{0:T(128)S(1)}, f32[64]{0:T(128)}, u32[]{:S(2)}) copy-start(f32[64]{0:T(128)} %iota_convert_fusion) | copy-start | bytes 772
  52.2 9.8 %copy-start.9 = (f32[32]{0:T(128)S(1)}, f32[32]{0:T(128)}, u32[]{:S(2)}) copy-start(f32[32]{0:T(128)} %multiply_exponential_fusion) | copy-start | bytes 388
  52.5 10.0 %copy-start.3 = (f32[64,8,32]{2,1,0:T(8,128)S(1)}, f32[64,8,32]{2,1,0:T(8,128)}, u32[]{:S(2)}) copy-start(f32[64,8,32]{2,1,0:T(8,128)} %get-tuple-element.69) | copy-start | bytes 196612
  52.5 10.0 %copy-start.4 = (f32[64,8,32]{2,1,0:T(8,128)S(1)}, f32[64,8,32]{2,1,0:T(8,128)}, u32[]{:S(2)}) copy-start(f32[64,8,32]{2,1,0:T(8,128)} %get-tuple-element.70) | copy-start | bytes 196612
  64.0 260.6 %all-to-all-start = ((bf16[64,8,576]{2,1,0:T(8,128)(2,1)}), bf16[64,8,576]{2,1,0:T(8,128)(2,1)S(1)}, u32[]{:S(2)}, u32[]{:S(2)}) async-start(bf16[64,8,576]{2,1,0:T(8,128)(2,1)} %copy.60), calls=%async_computation | async-start | bytes 1310720 | tf_op jit(solution)/shard_map/all_to_all | solution.py:95
  77.4 7.0 %copy-start.10 = (s32[4]{0:T(128)S(1)}, s32[4]{0:T(128)}, u32[]{:S(2)}) copy-start(s32[4]{0:T(128)} %param.21) | copy-start | bytes 52
  77.4 13.5 %copy-start.7 = (pred[4,32]{1,0:T(4,128)(4,1)S(1)}, pred[4,32]{1,0:T(4,128)(4,1)}, u32[]{:S(2)}) copy-start(pred[4,32]{1,0:T(4,128)(4,1)} %copy-done.6) | copy-start | bytes 388
  84.3 19.2 %collective-permute-start = (bf16[1,1,8,64,576]{4,3,2,0,1:T(8,128)(2,1)}, bf16[1,1,8,64,576]{4,3,2,0,1:T(8,128)(2,1)}, u32[]{:S(2)}, u32[]{:S(2)}) collective-permute-start(bf16[1,1,8,64,576]{4,3,2,0,1:T(8,128)(2,1)} %get-tuple-element.65), channel_id=1, source_target_pairs={{0,1},{1,2},{2,3},{3,4},{4,5},{5,6},{6,7},{7,8},{8,9},{9,10},{10,1... | collective-permute-start | bytes 1769480 | tf_op jit(solution)/shard_map/ppermute | solution.py:105
  84.8 20.8 %collective-permute-start.1 = (bf16[1,1,8,64,576]{4,3,2,0,1:T(8,128)(2,1)}, bf16[1,1,8,64,576]{4,3,2,0,1:T(8,128)(2,1)}, u32[]{:S(2)}, u32[]{:S(2)}) collective-permute-start(bf16[1,1,8,64,576]{4,3,2,0,1:T(8,128)(2,1)} %get-tuple-element.64), channel_id=1, source_target_pairs={{0,2},{1,3},{2,4},{3,5},{4,6},{5,7},{6,8},{7,9},{8,10},{9,11},{10,... | collective-permute-start | bytes 1769480 | tf_op jit(solution)/shard_map/ppermute | solution.py:105
  86.4 32.6 %collective-permute-start.2 = (bf16[1,1,8,64,576]{4,3,2,0,1:T(8,128)(2,1)}, bf16[1,1,8,64,576]{4,3,2,0,1:T(8,128)(2,1)}, u32[]{:S(2)}, u32[]{:S(2)}) collective-permute-start(bf16[1,1,8,64,576]{4,3,2,0,1:T(8,128)(2,1)} %get-tuple-element.63), channel_id=1, source_target_pairs={{0,3},{1,4},{2,5},{3,6},{4,7},{5,8},{6,9},{7,10},{8,11},{9,12},{10... | collective-permute-start | bytes 1769480 | tf_op jit(solution)/shard_map/ppermute | solution.py:105
  88.7 34.8 %collective-permute-start.3 = (bf16[1,1,8,64,576]{4,3,2,0,1:T(8,128)(2,1)}, bf16[1,1,8,64,576]{4,3,2,0,1:T(8,128)(2,1)}, u32[]{:S(2)}, u32[]{:S(2)}) collective-permute-start(bf16[1,1,8,64,576]{4,3,2,0,1:T(8,128)(2,1)} %get-tuple-element.62), channel_id=1, source_target_pairs={{0,4},{1,5},{2,6},{3,7},{4,8},{5,9},{6,10},{7,11},{8,12},{9,13},{1... | collective-permute-start | bytes 1769480 | tf_op jit(solution)/shard_map/ppermute | solution.py:105
  90.1 126.6 %collective-permute-start.4 = (bf16[1,1,8,64,576]{4,3,2,0,1:T(8,128)(2,1)}, bf16[1,1,8,64,576]{4,3,2,0,1:T(8,128)(2,1)}, u32[]{:S(2)}, u32[]{:S(2)}) collective-permute-start(bf16[1,1,8,64,576]{4,3,2,0,1:T(8,128)(2,1)} %get-tuple-element.61), channel_id=1, source_target_pairs={{0,5},{1,6},{2,7},{3,8},{4,9},{5,10},{6,11},{7,12},{8,13},{9,14},{... | collective-permute-start | bytes 1769480 | tf_op jit(solution)/shard_map/ppermute | solution.py:105
  103.6 115.1 %collective-permute-start.5 = (bf16[1,1,8,64,576]{4,3,2,0,1:T(8,128)(2,1)}, bf16[1,1,8,64,576]{4,3,2,0,1:T(8,128)(2,1)S(1)}, u32[]{:S(2)}, u32[]{:S(2)}) collective-permute-start(bf16[1,1,8,64,576]{4,3,2,0,1:T(8,128)(2,1)} %get-tuple-element.60), channel_id=1, source_target_pairs={{0,6},{1,7},{2,8},{3,9},{4,10},{5,11},{6,12},{7,13},{8,14},{9,15},... | collective-permute-start | bytes 1769480 | tf_op jit(solution)/shard_map/ppermute | solution.py:105
  105.6 129.5 %collective-permute-start.6 = (bf16[1,1,8,64,576]{4,3,2,0,1:T(8,128)(2,1)}, bf16[1,1,8,64,576]{4,3,2,0,1:T(8,128)(2,1)S(1)}, u32[]{:S(2)}, u32[]{:S(2)}) collective-permute-start(bf16[1,1,8,64,576]{4,3,2,0,1:T(8,128)(2,1)} %get-tuple-element.59), channel_id=1, source_target_pairs={{0,7},{1,8},{2,9},{3,10},{4,11},{5,12},{6,13},{7,14},{8,15},{9,0},... | collective-permute-start | bytes 1769480 | tf_op jit(solution)/shard_map/ppermute | solution.py:105
  119.0 148.6 %collective-permute-start.7 = (bf16[1,1,8,64,576]{4,3,2,0,1:T(8,128)(2,1)}, bf16[1,1,8,64,576]{4,3,2,0,1:T(8,128)(2,1)S(1)}, u32[]{:S(2)}, u32[]{:S(2)}) collective-permute-start(bf16[1,1,8,64,576]{4,3,2,0,1:T(8,128)(2,1)} %get-tuple-element.58), channel_id=1, source_target_pairs={{0,8},{1,9},{2,10},{3,11},{4,12},{5,13},{6,14},{7,15},{8,0},{9,1},... | collective-permute-start | bytes 1769480 | tf_op jit(solution)/shard_map/ppermute | solution.py:105
  123.5 146.3 %collective-permute-start.8 = (bf16[1,1,8,64,576]{4,3,2,0,1:T(8,128)(2,1)}, bf16[1,1,8,64,576]{4,3,2,0,1:T(8,128)(2,1)S(1)}, u32[]{:S(2)}, u32[]{:S(2)}) collective-permute-start(bf16[1,1,8,64,576]{4,3,2,0,1:T(8,128)(2,1)} %get-tuple-element.57), channel_id=1, source_target_pairs={{0,9},{1,10},{2,11},{3,12},{4,13},{5,14},{6,15},{7,0},{8,1},{9,2},... | collective-permute-start | bytes 1769480 | tf_op jit(solution)/shard_map/ppermute | solution.py:105
  216.7 74.7 %collective-permute-start.9 = (bf16[1,1,8,64,576]{4,3,2,0,1:T(8,128)(2,1)}, bf16[1,1,8,64,576]{4,3,2,0,1:T(8,128)(2,1)S(1)}, u32[]{:S(2)}, u32[]{:S(2)}) collective-permute-start(bf16[1,1,8,64,576]{4,3,2,0,1:T(8,128)(2,1)} %get-tuple-element.56), channel_id=1, source_target_pairs={{0,10},{1,11},{2,12},{3,13},{4,14},{5,15},{6,0},{7,1},{8,2},{9,3},... | collective-permute-start | bytes 1769480 | tf_op jit(solution)/shard_map/ppermute | solution.py:105
  218.7 92.3 %collective-permute-start.10 = (bf16[1,1,8,64,576]{4,3,2,0,1:T(8,128)(2,1)}, bf16[1,1,8,64,576]{4,3,2,0,1:T(8,128)(2,1)S(1)}, u32[]{:S(2)}, u32[]{:S(2)}) collective-permute-start(bf16[1,1,8,64,576]{4,3,2,0,1:T(8,128)(2,1)} %get-tuple-element.55), channel_id=1, source_target_pairs={{0,11},{1,12},{2,13},{3,14},{4,15},{5,0},{6,1},{7,2},{8,3},{9,4},{... | collective-permute-start | bytes 1769480 | tf_op jit(solution)/shard_map/ppermute | solution.py:105
  235.1 76.8 %collective-permute-start.11 = (bf16[1,1,8,64,576]{4,3,2,0,1:T(8,128)(2,1)}, bf16[1,1,8,64,576]{4,3,2,0,1:T(8,128)(2,1)S(1)}, u32[]{:S(2)}, u32[]{:S(2)}) collective-permute-start(bf16[1,1,8,64,576]{4,3,2,0,1:T(8,128)(2,1)} %get-tuple-element.54), channel_id=1, source_target_pairs={{0,12},{1,13},{2,14},{3,15},{4,0},{5,1},{6,2},{7,3},{8,4},{9,5},{1... | collective-permute-start | bytes 1769480 | tf_op jit(solution)/shard_map/ppermute | solution.py:105
  267.6 45.2 %collective-permute-start.12 = (bf16[1,1,8,64,576]{4,3,2,0,1:T(8,128)(2,1)S(1)}, bf16[1,1,8,64,576]{4,3,2,0,1:T(8,128)(2,1)S(1)}, u32[]{:S(2)}, u32[]{:S(2)}) collective-permute-start(bf16[1,1,8,64,576]{4,3,2,0,1:T(8,128)(2,1)S(1)} %get-tuple-element.53), channel_id=1, source_target_pairs={{0,13},{1,14},{2,15},{3,0},{4,1},{5,2},{6,3},{7,4},{8,5},{9,6},{10... | collective-permute-start | bytes 1769480 | tf_op jit(solution)/shard_map/ppermute | solution.py:105
  269.7 48.6 %collective-permute-start.13 = (bf16[1,1,8,64,576]{4,3,2,0,1:T(8,128)(2,1)S(1)}, bf16[1,1,8,64,576]{4,3,2,0,1:T(8,128)(2,1)S(1)}, u32[]{:S(2)}, u32[]{:S(2)}) collective-permute-start(bf16[1,1,8,64,576]{4,3,2,0,1:T(8,128)(2,1)S(1)} %get-tuple-element.66), channel_id=1, source_target_pairs={{0,14},{1,15},{2,0},{3,1},{4,2},{5,3},{6,4},{7,5},{8,6},{9,7},{10,... | collective-permute-start | bytes 1769480 | tf_op jit(solution)/shard_map/ppermute | solution.py:105
  291.3 32.4 %collective-permute-start.14 = (bf16[1,1,8,64,576]{4,3,2,0,1:T(8,128)(2,1)S(1)}, bf16[1,1,8,64,576]{4,3,2,0,1:T(8,128)(2,1)S(1)}, u32[]{:S(2)}, u32[]{:S(2)}) collective-permute-start(bf16[1,1,8,64,576]{4,3,2,0,1:T(8,128)(2,1)S(1)} %get-tuple-element.52), channel_id=1, source_target_pairs={{0,15},{1,0},{2,1},{3,2},{4,3},{5,4},{6,5},{7,6},{8,7},{9,8},{10,9... | collective-permute-start | bytes 1769480 | tf_op jit(solution)/shard_map/ppermute | solution.py:105
  324.7 97.7 %copy-start.11 = (u32[32]{0:T(128)S(1)}, u32[32]{0:T(128)}, u32[]{:S(2)}) copy-start(u32[32]{0:T(128)} %constant.291) | copy-start | bytes 388
  324.7 112.3 %copy-start.2 = (bf16[8,512,128]{2,1,0:T(8,128)(2,1)S(1)}, bf16[8,512,128]{2,1,0:T(8,128)(2,1)}, u32[]{:S(2)}) copy-start(bf16[8,512,128]{2,1,0:T(8,128)(2,1)} %param.16) | copy-start | bytes 3145732
  409.9 26.8 %all-to-all-start.2 = ((bf16[4,128,512]{2,0,1:T(4,128)(2,1)}), bf16[4,128,512]{2,0,1:T(4,128)(2,1)S(1)}, u32[]{:S(2)}, u32[]{:S(2)}) async-start(bf16[4,128,512]{2,0,1:T(4,128)(2,1)} %copy.69), calls=%async_computation.2 | async-start | bytes 1048576 | tf_op jit(solution)/shard_map/all_to_all | solution.py:130
  437.0 83.8 %copy-start.1 = (bf16[8,128,512]{2,1,0:T(8,128)(2,1)S(1)}, bf16[8,128,512]{2,1,0:T(8,128)(2,1)}, u32[]{:S(2)}) copy-start(bf16[8,128,512]{2,1,0:T(8,128)(2,1)} %param.15) | copy-start | bytes 3145732
